TPU v7x, 512 devices: a whole 4x8x8 slice. The times are simulated.
512 devices in a mesh: fsdp: 16 (over y, x_lo), ed: 32 (over x_hi, z, core).
Axes of the slice: x: 4 (x_hi: 2, x_lo: 2; x = x_hi * 2 + x_lo), y: 8, z: 8, core: 2. Of those that a mesh axis runs over, the one named last changes fastest.
Arguments:
- tokens: bfloat16 [9216, 6144], P('ed', 'fsdp'), may hold values from -6 to 6
- expert_ids: int32 [9216, 2], P('ed'), may hold values from 0 to 7, all different within a row; in each aligned block of 288 rows (0 to 287, 288 to 575, ...) at most 81 rows name the same one
- route_weights: float32 [9216, 2], P('ed'), may hold values from 0.1 to 1
- w_gate: bfloat16 [1, 6144, 8192], P(None, 'fsdp', 'ed'), may hold values from -0.078125 to 0.078125
- w_up: bfloat16 [1, 6144, 8192], P(None, 'fsdp', 'ed'), may hold values from -0.078125 to 0.078125
- w_down: bfloat16 [1, 8192, 6144], P(None, 'ed', 'fsdp'), may hold values from -0.0625 to 0.0625
Outputs:
- mixed: bfloat16 [9216, 6144], P('ed', 'fsdp')
Inputs may be any that keep to these rules, and one draw needn't show every extreme that they name: `expert_ids`: each row names two different experts. In each block of 288 rows that one index of ed holds, no expert is named by more than 81 rows, a bound that some block reaches.
All inputs are finite; a program needn't handle non-finite values.
Results may differ from a plain program's by a relative error of at most 0.025.
Values may be sent and summed in bfloat16 or wider, within the bound.
A program may use at most 64 MiB of HBM per device.

v0:
```python
import jax
import jax.numpy as jnp
from jax import lax
from jax.sharding import PartitionSpec as P

CAP = 81


def slot_match(routes, window, capacity):
    window_ids = jnp.arange(window, dtype=jnp.int32)
    routed = jnp.any(routes[:, :, None, :] == window_ids[None, None, :, None], axis=3)
    position = jnp.cumsum(routed.astype(jnp.int32), axis=1) - 1
    slot_ids = jnp.arange(capacity, dtype=jnp.int32)
    hits = routed[:, :, :, None] & (position[:, :, :, None] == slot_ids[None, None, None, :])
    return hits.astype(jnp.int32)


def take_block(block_rows, row_list):
    return jnp.take(block_rows, row_list, axis=0)


def pick_rows(blocks, routes, window, capacity):
    match = slot_match(routes, window, capacity)
    row_numbers = jnp.arange(blocks.shape[1], dtype=jnp.int32)
    source_row = jnp.sum(match * row_numbers[None, :, None, None], axis=1).reshape(
        blocks.shape[0], window * capacity
    )
    filled = jnp.sum(match, axis=1).reshape(blocks.shape[0], window * capacity)
    picked = jax.vmap(take_block)(blocks, source_row)
    picked = jnp.where(filled[:, :, None] > 0, picked, jnp.zeros_like(picked))
    return picked.reshape(blocks.shape[0], window, capacity, blocks.shape[2])


def combine_matrix(routes, weights, window, capacity):
    match = slot_match(routes[None], window, capacity)[0]
    window_ids = jnp.arange(window, dtype=jnp.int32)
    per_expert = jnp.sum(
        jnp.where(
            routes[:, None, :] == window_ids[None, :, None],
            weights[:, None, :],
            jnp.zeros_like(weights[:, None, :]),
        ),
        axis=2,
    )
    return (per_expert[:, :, None] * match.astype(weights.dtype)).reshape(
        routes.shape[0], window * capacity
    )


def local(tokens, expert_ids, route_weights, w_gate, w_up, w_down):
    window = w_gate.shape[0]
    features_dev = tokens.shape[1]
    own_slots = pick_rows(tokens[None], expert_ids[None], window, CAP)[0]
    selected = lax.all_gather(own_slots, "ed", axis=1, tiled=True)
    rows_full = lax.all_to_all(selected, "fsdp", split_axis=1, concat_axis=2, tiled=True)
    gate_part = jnp.einsum(
        "hnm,hmq->hnq",
        rows_full,
        lax.all_gather(w_gate, "fsdp", axis=1, tiled=True),
        preferred_element_type=jnp.float32,
    )
    up_part = jnp.einsum(
        "hnm,hmq->hnq",
        rows_full,
        lax.all_gather(w_up, "fsdp", axis=1, tiled=True),
        preferred_element_type=jnp.float32,
    )
    activation = (jax.nn.silu(gate_part) * up_part).astype(jnp.bfloat16)
    act_one = activation[0]

    def columns_out(shard_piece, first_col, act_one=act_one):
        return jnp.dot(act_one, shard_piece, preferred_element_type=jnp.float32)

    whole_rows = columns_out(lax.all_gather(w_down[0], "fsdp", axis=1, tiled=True), jnp.int32(0))
    outputs_list = [whole_rows.astype(jnp.bfloat16)]
    stacked = jnp.stack(outputs_list)
    exchanged = lax.all_to_all(stacked, "fsdp", split_axis=2, concat_axis=1, tiled=True)
    partial_out = exchanged.astype(jnp.float32)
    slot_out = lax.psum_scatter(
        partial_out.astype(jnp.bfloat16), "ed", scatter_dimension=1, tiled=True
    ).astype(jnp.float32)
    weights_matrix = combine_matrix(expert_ids, route_weights, window, CAP)
    mixed = jnp.dot(
        weights_matrix,
        slot_out.reshape(window * CAP, features_dev),
        precision=lax.Precision.HIGHEST,
        preferred_element_type=jnp.float32,
    )
    return mixed.astype(jnp.bfloat16)


def solution(mesh):
    return jax.shard_map(
        local,
        mesh=mesh,
        in_specs=(
            P("ed", "fsdp"),
            P("ed", None),
            P("ed", None),
            P(None, "fsdp", "ed"),
            P(None, "fsdp", "ed"),
            P(None, "ed", "fsdp"),
        ),
        out_specs=P("ed", "fsdp"),
        check_vma=False,
    )
```

profile of v0, /device:TPU:1, one launch (start us, length us, event | category | flops | bytes accessed | tf_op | source)
XLA Modules:
  0.0 640.9 jit_solution(6663339600788899471)
XLA Ops:
  6.5 0.0 copy-start
  6.5 0.0 all-gather.6.cloned.1.call-start
  6.5 0.7 fusion.27
  7.3 0.3 reduce-window.6
  7.6 0.2 slice_reduce_fusion
  7.8 0.2 reduce-window.9
  8.0 0.1 broadcast.258
  8.1 3.0 convert_reduce_fusion
  11.1 0.0 copy-done
  11.1 1.3 gather_fusion
  12.4 0.1 fusion.22
  12.5 0.7 copy.18
  13.3 0.0 all-gather.6.cloned.1.call-update
  13.3 0.0 all-gather.8.cloned.1.call-start
  13.4 0.7 all-gather.8.cloned.1.call-update
  14.1 0.0 all-gather.10.cloned.1.call-start
  14.1 0.7 all-gather.10.cloned.1.call-update
  14.8 0.0 all-gather.12.cloned.1.call-start
  14.8 0.5 all-gather.12.cloned.1.call-update
  15.4 96.3 %all-gather.6.cloned.1.call-done = bf16[1,2592,384]{2,0,1:T(2,128)(2,1)} async-done(((bf16[1,81,384]{2,0,1:T(2,128)(2,1)}), bf16[1,2592,384]{2,0,1:T(2,128)(2,1)}) %all-gather.6.cloned.1.call-update) | async-done | bytes 1990672 | tf_op jit(solution)/shard_map/all_gather | solution.py:54
  111.6 0.5 broadcast.283
  112.2 15.8 %reduce.14 = bf16[2592,384]{1,0:T(8,128)(2,1)S(1)} reduce(bf16[2592,1,384]{2,1,0:T(2,128)(2,1)} %bitcast.80, bf16[]{:T(256)} %broadcast.283), dimensions={1}, to_apply=%bitcast.61.reduce_sub_computation | reduce | bytes 3981314
  128.0 1.6 reshape.463
  129.6 71.7 %all_to_all.33 = bf16[16,2,31104]{2,1,0:T(2,128)(2,1)S(1)} all-to-all(bf16[16,2,31104]{2,1,0:T(2,128)(2,1)} %reshape.463), channel_id=1, replica_groups=mesh['fsdp'=16,'ed'=32] {'fsdp'}, dimensions={0} | all-to-all | bytes 3981312 | tf_op jit(solution)/shard_map/all_to_all | solution.py:55
  201.2 8.9 %reshape.464 = bf16[2592,1,384]{2,1,0:T(2,128)(2,1)} reshape(bf16[16,2,31104]{2,1,0:T(2,128)(2,1)S(1)} %all_to_all.33) | data formatting | bytes 3981312
  210.2 17.6 %bitcast_reduce_fusion = bf16[2592,384]{1,0:T(8,128)(2,1)} fusion(bf16[2592,1,384]{2,1,0:T(2,128)(2,1)} %reshape.464), kind=kLoop, calls=%fused_computation.46 | loop fusion | bytes 3981312 | tf_op jit(solution)/shard_map/all_to_all | solution.py:55
  227.8 1.8 all_to_all.25
  229.5 0.3 copy.29
  229.8 0.2 pad.7
  230.0 0.5 copy.26
  230.6 0.0 all-gather.8.cloned.1.call-done
  230.6 2.7 fusion.5
  233.3 66.1 %all-gather.10.cloned.1.call-done = bf16[1,6144,256]{2,1,0:T(8,128)(2,1)} async-done(((bf16[1,384,256]{2,1,0:T(8,128)(2,1)}), bf16[1,6144,256]{2,1,0:T(8,128)(2,1)}) %all-gather.10.cloned.1.call-update) | async-done | bytes 3145744 | tf_op jit(solution)/shard_map/all_gather | solution.py:65
  299.3 85.3 %all-gather.12.cloned.1.call-done = bf16[1,256,6144]{2,1,0:T(8,128)(2,1)} async-done(((bf16[1,256,384]{2,1,0:T(8,128)(2,1)}), bf16[1,256,6144]{2,1,0:T(8,128)(2,1)}) %all-gather.12.cloned.1.call-update) | async-done | bytes 3145744 | tf_op jit(solution)/shard_map/all_gather | solution.py:74
  384.6 6.5 %fusion.1 = bf16[1,162,6144]{2,1,0:T(8,128)(2,1)} fusion(bf16[1,256,6144]{2,1,0:T(8,128)(2,1)} %all-gather.12.cloned.1.call-done, bf16[162,6144]{1,0:T(8,128)(2,1)S(1)} %bitcast.74, bf16[1,6144,256]{2,1,0:T(8,128)(2,1)} %all-gather.10.cloned.1.call-done, f32[162,256]{1,0:T(8,128)S(1)} %fusion.5), kind=kOutput, calls=%fused_computation.2 | convolution fusion | flops 1020460032 | bytes 10438656 | tf_op jit(solution)/shard_map/dot_general | solution.py:72
  391.1 13.7 %copy.20 = bf16[1,162,6144]{1,0,2:T(2,128)(2,1)} copy(bf16[1,162,6144]{2,1,0:T(8,128)(2,1)} %fusion.1) | data formatting | bytes 3981312 | tf_op jit(solution)/shard_map/stack | solution.py:76
  404.8 34.6 %reduce.15 = bf16[6144,162]{1,0:T(8,128)(2,1)S(1)} reduce(bf16[6144,1,162]{2,1,0:T(2,128)(2,1)} %bitcast.71, bf16[]{:T(256)} %broadcast.283), dimensions={1}, to_apply=%bitcast.63.reduce_sub_computation | reduce | bytes 3981314
  439.4 6.9 %reshape.465 = bf16[16,2,31104]{2,1,0:T(2,128)(2,1)} reshape(bf16[6144,162]{1,0:T(8,128)(2,1)S(1)} %reduce.15) | data formatting | bytes 3981312
  446.4 4.2 all-to-all-start.1
  450.6 0.0 copy-done.2
  450.6 0.0 copy-done.3
  450.7 42.9 %all-to-all-done.1 = bf16[16,2,31104]{2,1,0:T(2,128)(2,1)S(1)} async-done(((bf16[16,2,31104]{2,1,0:T(2,128)(2,1)}), bf16[16,2,31104]{2,1,0:T(2,128)(2,1)S(1)}, u32[]{:S(2)}, u32[]{:S(2)}) %all-to-all-start.1) | async-done | bytes 1990688 | tf_op jit(solution)/shard_map/all_to_all | solution.py:77
  493.5 12.1 %reshape.466 = bf16[6144,1,162]{2,1,0:T(2,128)(2,1)} reshape(bf16[16,2,31104]{2,1,0:T(2,128)(2,1)S(1)} %all-to-all-done.1) | data formatting | bytes 3981312
  505.6 13.8 %copy.21 = bf16[1,162,6144]{2,1,0:T(8,128)(2,1)S(1)} copy(bf16[1,162,6144]{1,0,2:T(2,128)(2,1)} %bitcast.72) | data formatting | bytes 3981312 | tf_op jit(solution)/shard_map/all_to_all | solution.py:77
  519.4 0.4 copy.27
  519.8 0.2 bitcast_bitcast_fusion
  520.0 0.4 copy.22
  520.5 0.0 copy-start.1
  520.5 1.6 all_to_all.30
  522.0 81.8 %fusion = bf16[96,384]{1,0:T(8,128)(2,1)S(1)} fusion(bf16[1,2592,384]{2,1,0:T(8,128)(2,1)} %all_to_all.30), kind=kCustom, calls=%all-reduce-scatter | all-reduce-scatter fusion | flops 1179649 | bytes 2066432
  603.9 3.5 collective-permute-start
  607.5 1.3 collective-permute-start.1
  608.8 1.3 collective-permute-start.2
  610.1 1.3 collective-permute-start.3
  611.4 16.7 %collective-permute-start.4 = (bf16[81,384]{1,0:T(8,128)(2,1)S(1)}, bf16[81,384]{1,0:T(8,128)(2,1)S(1)}, u32[]{:S(2)}, u32[]{:S(2)}) collective-permute-start(bf16[81,384]{1,0:T(8,128)(2,1)S(1)} %slice.16), channel_id=1, source_target_pairs={{0,5},{1,6},{2,7},{3,8},{4,9},{5,10},{6,11},{7,12},{8,13},{9,14},{... | collective-permute-start | bytes 186632
  628.1 1.7 convert_multiply_fusion
  629.8 1.3 dynamic-slice.4
  631.7 0.0 collective-permute-done.4
  631.7 0.0 collective-permute-done
  631.7 0.0 collective-permute-done.1
  631.7 0.0 collective-permute-done.2
  631.7 0.0 collective-permute-done.3
  631.8 1.6 concatenate.3
  633.4 1.0 convolution_convert_fusion.1
  (15 shorter events, 0.2 us)
Async XLA Ops:
  6.5 4.6 copy-start
  6.5 105.1 %all-gather.6.cloned.1.call-start = ((), (), s32[]{:S(2)}) async-start(), calls=%async_computation.2 | async-start | bytes 4105728 | tf_op jit(solution)/shard_map/all_gather | solution.py:54
  13.3 217.3 %all-gather.8.cloned.1.call-start = ((), (), s32[]{:S(2)}) async-start(), calls=%async_computation.3 | async-start | bytes 3342336 | tf_op jit(solution)/shard_map/all_gather | solution.py:59
  14.1 285.3 %all-gather.10.cloned.1.call-start = ((), (), s32[]{:S(2)}) async-start(), calls=%async_computation.4 | async-start | bytes 3342336 | tf_op jit(solution)/shard_map/all_gather | solution.py:65
  14.8 369.8 %all-gather.12.cloned.1.call-start = ((), (), s32[]{:S(2)}) async-start(), calls=%async_computation.5 | async-start | bytes 3342336 | tf_op jit(solution)/shard_map/all_gather | solution.py:74
  446.4 4.2 copy-start.2
  446.4 4.3 copy-start.3
  446.4 47.1 %all-to-all-start.1 = ((bf16[16,2,31104]{2,1,0:T(2,128)(2,1)}), bf16[16,2,31104]{2,1,0:T(2,128)(2,1)S(1)}, u32[]{:S(2)}, u32[]{:S(2)}) async-start(bf16[16,2,31104]{2,1,0:T(2,128)(2,1)} %reshape.465), calls=%async_computation.1 | async-start | bytes 3981312 | tf_op jit(solution)/shard_map/all_to_all | solution.py:77
  520.5 113.9 %copy-start.1 = (bf16[288,384]{1,0:T(8,128)(2,1)S(1)}, bf16[288,384]{1,0:T(8,128)(2,1)}, u32[]{:S(2)}) copy-start(bf16[288,384]{1,0:T(8,128)(2,1)} %param.6) | copy-start | bytes 663556
  603.9 27.8 %collective-permute-start = (bf16[96,384]{1,0:T(8,128)(2,1)S(1)}, bf16[96,384]{1,0:T(8,128)(2,1)S(1)}, u32[]{:S(2)}, u32[]{:S(2)}) collective-permute-start(bf16[96,384]{1,0:T(8,128)(2,1)S(1)} %fusion), channel_id=1, source_target_pairs={{0,1},{1,2},{2,3},{3,4},{4,5},{5,6},{6,7},{7,8},{8,9},{9,10},{10,1... | collective-permute-start | bytes 221192
  607.5 24.3 %collective-permute-start.1 = (bf16[96,384]{1,0:T(8,128)(2,1)S(1)}, bf16[96,384]{1,0:T(8,128)(2,1)S(1)}, u32[]{:S(2)}, u32[]{:S(2)}) collective-permute-start(bf16[96,384]{1,0:T(8,128)(2,1)S(1)} %fusion), channel_id=1, source_target_pairs={{0,2},{1,3},{2,4},{3,5},{4,6},{5,7},{6,8},{7,9},{8,10},{9,11},{10,... | collective-permute-start | bytes 221192
  608.8 23.0 %collective-permute-start.2 = (bf16[96,384]{1,0:T(8,128)(2,1)S(1)}, bf16[96,384]{1,0:T(8,128)(2,1)S(1)}, u32[]{:S(2)}, u32[]{:S(2)}) collective-permute-start(bf16[96,384]{1,0:T(8,128)(2,1)S(1)} %fusion), channel_id=1, source_target_pairs={{0,3},{1,4},{2,5},{3,6},{4,7},{5,8},{6,9},{7,10},{8,11},{9,12},{10... | collective-permute-start | bytes 221192
  610.1 21.7 %collective-permute-start.3 = (bf16[96,384]{1,0:T(8,128)(2,1)S(1)}, bf16[96,384]{1,0:T(8,128)(2,1)S(1)}, u32[]{:S(2)}, u32[]{:S(2)}) collective-permute-start(bf16[96,384]{1,0:T(8,128)(2,1)S(1)} %fusion), channel_id=1, source_target_pairs={{0,4},{1,5},{2,6},{3,7},{4,8},{5,9},{6,10},{7,11},{8,12},{9,13},{1... | collective-permute-start | bytes 221192
  611.4 20.3 %collective-permute-start.4 = (bf16[81,384]{1,0:T(8,128)(2,1)S(1)}, bf16[81,384]{1,0:T(8,128)(2,1)S(1)}, u32[]{:S(2)}, u32[]{:S(2)}) collective-permute-start(bf16[81,384]{1,0:T(8,128)(2,1)S(1)} %slice.16), channel_id=1, source_target_pairs={{0,5},{1,6},{2,7},{3,8},{4,9},{5,10},{6,11},{7,12},{8,13},{9,14},{... | collective-permute-start | bytes 186632
Sparse Core Ops, SparseCore 0:
  13.4 98.1 all-gather.5
  113.7 100.7 all-gather.7
  216.6 82.7 all-gather.9
  301.3 83.2 all-gather.11
where the time goes:
time: 642 us; the launch traced here: 641 us
  waiting for transfers between devices  292 us (45%)
  blocking collectives  154 us (24%)
  local copies, waits for them, and re-layouts  85.7 us (13%)
  other arithmetic  56.5 us (9%)
  starting transfers between devices  28.5 us (4%)
  between operations  14.1 us (2%)
  matrix products  10.2 us (2%)
    all_gather x1, waiting for transfers between devices, local(): selected = lax.all_gather(own_slots, 'ed', axis=1, tiled=True)  96.3 us
    all_gather x1, waiting for transfers between devices, local(): lax.all_gather(w_down[0], 'fsdp', axis=1, tiled=True)  85.3 us
    unnamed x1, blocking collectives  81.8 us
    all_to_all x1, blocking collectives, local(): lax.all_to_all(selected, 'fsdp', split_axis=1, concat_axis=2, tiled=True)  71.7 us
    all_gather x1, waiting for transfers between devices, local(): lax.all_gather(w_up, 'fsdp', axis=1, tiled=True)  66.1 us
    unnamed x2, other arithmetic  50.5 us
    all_to_all x1, waiting for transfers between devices, local(): lax.all_to_all(stacked, 'fsdp', split_axis=2, concat_axis=1, tiled=True)  42.9 us
    unnamed x19, local copies, waits for them, and re-layouts  34.1 us
  transfers between devices with their start and end apart: 10, of which 4 were waited for; matrix products, arithmetic and copies ran while one was open for 8% of the time, Pallas kernels for 0%

commit v1 on v0

--- a/solution.py
+++ b/solution.py
@@ -1,9 +1,19 @@
+import functools
 import jax
 import jax.numpy as jnp
 from jax import lax
 from jax.sharding import PartitionSpec as P
 
 CAP = 81
+
+
+def patch_show(v0, net_axis):
+    even = jax.lax.all_to_all(jnp.stack(jax.lax.axis_size(net_axis) * [v0], axis=0), net_axis, 0, 0)
+    x_new = jnp.concatenate(even, axis=1)
+    return x_new
+
+
+proceed_the_clusters = functools.partial(patch_show, net_axis="ed")
 
 
 def slot_match(routes, window, capacity):
@@ -51,7 +61,7 @@
     window = w_gate.shape[0]
     features_dev = tokens.shape[1]
     own_slots = pick_rows(tokens[None], expert_ids[None], window, CAP)[0]
-    selected = lax.all_gather(own_slots, "ed", axis=1, tiled=True)
+    selected = proceed_the_clusters(own_slots)
     rows_full = lax.all_to_all(selected, "fsdp", split_axis=1, concat_axis=2, tiled=True)
     gate_part = jnp.einsum(
         "hnm,hmq->hnq",

time: 642 us -> 562 us (0.88)
  waiting for transfers between devices: 292 us -> 202 us
  starting transfers between devices: 28.5 us -> 42.9 us
  blocking collectives: 154 us -> 140 us
  local copies, waits for them, and re-layouts: 85.7 us -> 94.4 us
    all_gather x1 -> x0, waiting for transfers between devices: 96.3 us -> none  [local(): selected = lax.all_gather(own_slots, 'ed', axis=1, tiled=True)]
    all_to_all x0 -> x1, waiting for transfers between devices: none -> 51.1 us  [patch_show(): jax.lax.all_to_all(jnp.stack(jax.lax.axis_size(net_axis) * [v0], axis=0),...]
    all_gather x1, waiting for transfers between devices: 66.1 us -> 21.7 us  [local(): lax.all_gather(w_up, 'fsdp', axis=1, tiled=True)]
    all_to_all x0 -> x1, starting transfers between devices: none -> 14.4 us  [patch_show(): jax.lax.all_to_all(jnp.stack(jax.lax.axis_size(net_axis) * [v0], axis=0),...]
    all_to_all x1, blocking collectives: 71.7 us -> 58.5 us  [local(): lax.all_to_all(selected, 'fsdp', split_axis=1, concat_axis=2, tiled=True)]
    reshape x0 -> x1, local copies, waits for them, and re-layouts: none -> 7.92 us  [patch_show(): x_new = jnp.concatenate(even, axis=1)]
  transfers between devices with their start and end apart: 10 -> 10, of which waited for: 4 -> 4; matrix products, arithmetic and copies ran while one was open for 8% -> 12% of each run, Pallas kernels for 0% -> 0%
where the time goes in v1:
time: 562 us; the launch traced here: 561 us
  waiting for transfers between devices  202 us (36%)
  blocking collectives  140 us (25%)
  local copies, waits for them, and re-layouts  94.4 us (17%)
  other arithmetic  56.5 us (10%)
  starting transfers between devices  42.9 us (8%)
  between operations  14 us (2%)
  matrix products  10.4 us (2%)
    all_gather x1, waiting for transfers between devices, local(): lax.all_gather(w_down[0], 'fsdp', axis=1, tiled=True)  84.3 us
    unnamed x1, blocking collectives  81.8 us
    all_to_all x1, blocking collectives, local(): lax.all_to_all(selected, 'fsdp', split_axis=1, concat_axis=2, tiled=True)  58.5 us
    all_to_all x1, waiting for transfers between devices, patch_show(): jax.lax.all_to_all(jnp.stack(jax.lax.axis_size(net_axis) * [v0], axis=0),...  51.1 us
    unnamed x2, other arithmetic  50.5 us
    all_to_all x1, waiting for transfers between devices, local(): lax.all_to_all(stacked, 'fsdp', split_axis=2, concat_axis=1, tiled=True)  42.9 us
    unnamed x19, local copies, waits for them, and re-layouts  34.1 us
    unnamed x5, starting transfers between devices  24.1 us
  transfers between devices with their start and end apart: 10, of which 4 were waited for; matrix products, arithmetic and copies ran while one was open for 12% of the time, Pallas kernels for 0%

profile of v1, /device:TPU:1, one launch (start us, length us, event | category | flops | bytes accessed | tf_op | source)
XLA Modules:
  0.0 560.6 jit_solution(11562746356790680400)
XLA Ops:
  6.5 0.0 copy-start
  6.5 0.0 all-gather.5.cloned.1.call-start
  6.5 0.7 all-gather.5.cloned.1.call-update
  7.3 0.0 all-gather.7.cloned.1.call-start
  7.3 0.7 all-gather.7.cloned.1.call-update
  8.0 0.7 fusion.26
  8.7 0.3 reduce-window.6
  9.1 0.2 slice_reduce_fusion
  9.3 0.2 reduce-window.9
  9.4 0.1 broadcast.242
  9.6 3.0 convert_reduce_fusion
  12.6 0.0 copy-done
  12.6 1.3 gather_fusion
  13.9 0.1 select_select_fusion
  14.0 1.5 stack.6
  15.5 14.4 %all-to-all-start = ((bf16[32,1,81,384]{3,2,1,0:T(8,128)(2,1)}), bf16[32,1,81,384]{3,2,1,0:T(8,128)(2,1)S(1)}, u32[]{:S(2)}, u32[]{:S(2)}) async-start(bf16[32,1,81,384]{3,2,1,0:T(8,128)(2,1)} %stack.6), calls=%async_computation | async-start | bytes 4325376 | tf_op jit(solution)/shard_map/all_to_all | solution.py:11
  30.0 0.0 all-gather.9.cloned.1.call-start
  30.0 0.7 all-gather.9.cloned.1.call-update
  30.7 51.1 %all-to-all-done = bf16[32,1,81,384]{3,2,1,0:T(8,128)(2,1)S(1)} async-done(((bf16[32,1,81,384]{3,2,1,0:T(8,128)(2,1)}), bf16[32,1,81,384]{3,2,1,0:T(8,128)(2,1)S(1)}, u32[]{:S(2)}, u32[]{:S(2)}) %all-to-all-start) | async-done | bytes 1990688 | tf_op jit(solution)/shard_map/all_to_all | solution.py:11
  81.8 7.9 %reshape.449 = bf16[1,2592,384]{2,0,1:T(2,128)(2,1)} reshape(bf16[32,1,81,384]{3,2,1,0:T(8,128)(2,1)S(1)} %all-to-all-done) | data formatting | bytes 3981312 | tf_op jit(solution)/shard_map/reshape | solution.py:12
  89.7 0.5 broadcast.267
  90.2 15.8 %reduce.14 = bf16[2592,384]{1,0:T(8,128)(2,1)S(1)} reduce(bf16[2592,1,384]{2,1,0:T(2,128)(2,1)} %bitcast.71, bf16[]{:T(256)} %broadcast.267), dimensions={1}, to_apply=%bitcast.57.reduce_sub_computation | reduce | bytes 3981314
  106.1 1.6 reshape.457
  107.7 58.5 %all_to_all.38 = bf16[16,2,31104]{2,1,0:T(2,128)(2,1)S(1)} all-to-all(bf16[16,2,31104]{2,1,0:T(2,128)(2,1)} %reshape.457), channel_id=1, replica_groups=mesh['fsdp'=16,'ed'=32] {'fsdp'}, dimensions={0} | all-to-all | bytes 3981312 | tf_op jit(solution)/shard_map/all_to_all | solution.py:65
  166.1 8.9 %reshape.458 = bf16[2592,1,384]{2,1,0:T(2,128)(2,1)} reshape(bf16[16,2,31104]{2,1,0:T(2,128)(2,1)S(1)} %all_to_all.38) | data formatting | bytes 3981312
  175.0 17.6 %bitcast_reduce_fusion = bf16[2592,384]{1,0:T(8,128)(2,1)} fusion(bf16[2592,1,384]{2,1,0:T(2,128)(2,1)} %reshape.458), kind=kLoop, calls=%fused_computation.45 | loop fusion | bytes 3981312 | tf_op jit(solution)/shard_map/all_to_all | solution.py:65
  192.6 1.8 all_to_all.29
  194.4 0.3 copy.29
  194.7 0.2 pad.7
  194.9 0.5 copy.26
  195.4 0.0 all-gather.5.cloned.1.call-done
  195.5 2.7 fusion.5
  198.2 21.7 %all-gather.7.cloned.1.call-done = bf16[1,6144,256]{2,1,0:T(8,128)(2,1)} async-done(((bf16[1,384,256]{2,1,0:T(8,128)(2,1)}), bf16[1,6144,256]{2,1,0:T(8,128)(2,1)}) %all-gather.7.cloned.1.call-update) | async-done | bytes 3145744 | tf_op jit(solution)/shard_map/all_gather | solution.py:75
  219.9 84.3 %all-gather.9.cloned.1.call-done = bf16[1,256,6144]{2,1,0:T(8,128)(2,1)} async-done(((bf16[1,256,384]{2,1,0:T(8,128)(2,1)}), bf16[1,256,6144]{2,1,0:T(8,128)(2,1)}) %all-gather.9.cloned.1.call-update) | async-done | bytes 3145744 | tf_op jit(solution)/shard_map/all_gather | solution.py:84
  304.2 6.6 %fusion.1 = bf16[1,162,6144]{2,1,0:T(8,128)(2,1)} fusion(bf16[1,256,6144]{2,1,0:T(8,128)(2,1)} %all-gather.9.cloned.1.call-done, bf16[162,6144]{1,0:T(8,128)(2,1)S(1)} %bitcast.70, bf16[1,6144,256]{2,1,0:T(8,128)(2,1)} %all-gather.7.cloned.1.call-done, f32[162,256]{1,0:T(8,128)S(1)} %fusion.5), kind=kOutput, calls=%fused_computation.2 | convolution fusion | flops 1020460032 | bytes 10438656 | tf_op jit(solution)/shard_map/dot_general | solution.py:82
  310.9 13.7 %copy.20 = bf16[1,162,6144]{1,0,2:T(2,128)(2,1)} copy(bf16[1,162,6144]{2,1,0:T(8,128)(2,1)} %fusion.1) | data formatting | bytes 3981312 | tf_op jit(solution)/shard_map/stack | solution.py:86
  324.6 34.6 %reduce.15 = bf16[6144,162]{1,0:T(8,128)(2,1)S(1)} reduce(bf16[6144,1,162]{2,1,0:T(2,128)(2,1)} %bitcast.67, bf16[]{:T(256)} %broadcast.267), dimensions={1}, to_apply=%bitcast.59.reduce_sub_computation | reduce | bytes 3981314
  359.2 6.9 %reshape.459 = bf16[16,2,31104]{2,1,0:T(2,128)(2,1)} reshape(bf16[6144,162]{1,0:T(8,128)(2,1)S(1)} %reduce.15) | data formatting | bytes 3981312
  366.1 4.2 all-to-all-start.2
  370.3 0.0 copy-done.2
  370.3 0.0 copy-done.3
  370.4 42.9 %all-to-all-done.2 = bf16[16,2,31104]{2,1,0:T(2,128)(2,1)S(1)} async-done(((bf16[16,2,31104]{2,1,0:T(2,128)(2,1)}), bf16[16,2,31104]{2,1,0:T(2,128)(2,1)S(1)}, u32[]{:S(2)}, u32[]{:S(2)}) %all-to-all-start.2) | async-done | bytes 1990688 | tf_op jit(solution)/shard_map/all_to_all | solution.py:87
  413.2 12.1 %reshape.460 = bf16[6144,1,162]{2,1,0:T(2,128)(2,1)} reshape(bf16[16,2,31104]{2,1,0:T(2,128)(2,1)S(1)} %all-to-all-done.2) | data formatting | bytes 3981312
  425.3 13.8 %copy.21 = bf16[1,162,6144]{2,1,0:T(8,128)(2,1)S(1)} copy(bf16[1,162,6144]{1,0,2:T(2,128)(2,1)} %bitcast.68) | data formatting | bytes 3981312 | tf_op jit(solution)/shard_map/all_to_all | solution.py:87
  439.1 0.4 copy.27
  439.5 0.2 bitcast_bitcast_fusion
  439.7 0.4 copy.22
  440.2 0.0 copy-start.1
  440.2 1.6 all_to_all.34
  441.7 81.8 %fusion = bf16[96,384]{1,0:T(8,128)(2,1)S(1)} fusion(bf16[1,2592,384]{2,1,0:T(8,128)(2,1)} %all_to_all.34), kind=kCustom, calls=%all-reduce-scatter | all-reduce-scatter fusion | flops 1179649 | bytes 2066432
  523.6 3.5 collective-permute-start
  527.2 1.3 collective-permute-start.1
  528.5 1.3 collective-permute-start.2
  529.8 1.3 collective-permute-start.3
  531.1 16.7 %collective-permute-start.4 = (bf16[81,384]{1,0:T(8,128)(2,1)S(1)}, bf16[81,384]{1,0:T(8,128)(2,1)S(1)}, u32[]{:S(2)}, u32[]{:S(2)}) collective-permute-start(bf16[81,384]{1,0:T(8,128)(2,1)S(1)} %slice.16), channel_id=1, source_target_pairs={{0,5},{1,6},{2,7},{3,8},{4,9},{5,10},{6,11},{7,12},{8,13},{9,14},{... | collective-permute-start | bytes 186632
  547.8 1.7 convert_multiply_fusion
  549.5 1.3 dynamic-slice.4
  551.4 0.0 collective-permute-done.4
  551.4 0.0 collective-permute-done
  551.4 0.0 collective-permute-done.1
  551.5 0.0 collective-permute-done.2
  551.5 0.0 collective-permute-done.3
  551.5 1.6 concatenate.3
  553.1 1.0 convolution_convert_fusion.1
  (15 shorter events, 0.2 us)
Async XLA Ops:
  6.5 6.0 %copy-start = (bf16[288,384]{1,0:T(8,128)(2,1)S(1)}, bf16[288,384]{1,0:T(8,128)(2,1)}, u32[]{:S(2)}) copy-start(bf16[288,384]{1,0:T(8,128)(2,1)} %param.6) | copy-start | bytes 663556
  6.5 188.9 %all-gather.5.cloned.1.call-start = ((), (), s32[]{:S(2)}) async-start(), calls=%async_computation.3 | async-start | bytes 3342336 | tf_op jit(solution)/shard_map/all_gather | solution.py:69
  7.3 212.7 %all-gather.7.cloned.1.call-start = ((), (), s32[]{:S(2)}) async-start(), calls=%async_computation.4 | async-start | bytes 3342336 | tf_op jit(solution)/shard_map/all_gather | solution.py:75
  15.5 66.3 %all-to-all-start = ((bf16[32,1,81,384]{3,2,1,0:T(8,128)(2,1)}), bf16[32,1,81,384]{3,2,1,0:T(8,128)(2,1)S(1)}, u32[]{:S(2)}, u32[]{:S(2)}) async-start(bf16[32,1,81,384]{3,2,1,0:T(8,128)(2,1)} %stack.6), calls=%async_computation | async-start | bytes 4325376 | tf_op jit(solution)/shard_map/all_to_all | solution.py:11
  30.0 274.3 %all-gather.9.cloned.1.call-start = ((), (), s32[]{:S(2)}) async-start(), calls=%async_computation.5 | async-start | bytes 3342336 | tf_op jit(solution)/shard_map/all_gather | solution.py:84
  366.1 4.2 copy-start.2
  366.1 4.3 copy-start.3
  366.1 47.1 %all-to-all-start.2 = ((bf16[16,2,31104]{2,1,0:T(2,128)(2,1)}), bf16[16,2,31104]{2,1,0:T(2,128)(2,1)S(1)}, u32[]{:S(2)}, u32[]{:S(2)}) async-start(bf16[16,2,31104]{2,1,0:T(2,128)(2,1)} %reshape.459), calls=%async_computation.2 | async-start | bytes 3981312 | tf_op jit(solution)/shard_map/all_to_all | solution.py:87
  440.2 113.9 %copy-start.1 = (bf16[288,384]{1,0:T(8,128)(2,1)S(1)}, bf16[288,384]{1,0:T(8,128)(2,1)}, u32[]{:S(2)}) copy-start(bf16[288,384]{1,0:T(8,128)(2,1)} %param.6) | copy-start | bytes 663556
  523.6 27.8 %collective-permute-start = (bf16[96,384]{1,0:T(8,128)(2,1)S(1)}, bf16[96,384]{1,0:T(8,128)(2,1)S(1)}, u32[]{:S(2)}, u32[]{:S(2)}) collective-permute-start(bf16[96,384]{1,0:T(8,128)(2,1)S(1)} %fusion), channel_id=1, source_target_pairs={{0,1},{1,2},{2,3},{3,4},{4,5},{5,6},{6,7},{7,8},{8,9},{9,10},{10,1... | collective-permute-start | bytes 221192
  527.2 24.3 %collective-permute-start.1 = (bf16[96,384]{1,0:T(8,128)(2,1)S(1)}, bf16[96,384]{1,0:T(8,128)(2,1)S(1)}, u32[]{:S(2)}, u32[]{:S(2)}) collective-permute-start(bf16[96,384]{1,0:T(8,128)(2,1)S(1)} %fusion), channel_id=1, source_target_pairs={{0,2},{1,3},{2,4},{3,5},{4,6},{5,7},{6,8},{7,9},{8,10},{9,11},{10,... | collective-permute-start | bytes 221192
  528.5 23.0 %collective-permute-start.2 = (bf16[96,384]{1,0:T(8,128)(2,1)S(1)}, bf16[96,384]{1,0:T(8,128)(2,1)S(1)}, u32[]{:S(2)}, u32[]{:S(2)}) collective-permute-start(bf16[96,384]{1,0:T(8,128)(2,1)S(1)} %fusion), channel_id=1, source_target_pairs={{0,3},{1,4},{2,5},{3,6},{4,7},{5,8},{6,9},{7,10},{8,11},{9,12},{10... | collective-permute-start | bytes 221192
  529.8 21.7 %collective-permute-start.3 = (bf16[96,384]{1,0:T(8,128)(2,1)S(1)}, bf16[96,384]{1,0:T(8,128)(2,1)S(1)}, u32[]{:S(2)}, u32[]{:S(2)}) collective-permute-start(bf16[96,384]{1,0:T(8,128)(2,1)S(1)} %fusion), channel_id=1, source_target_pairs={{0,4},{1,5},{2,6},{3,7},{4,8},{5,9},{6,10},{7,11},{8,12},{9,13},{1... | collective-permute-start | bytes 221192
  531.1 20.3 %collective-permute-start.4 = (bf16[81,384]{1,0:T(8,128)(2,1)S(1)}, bf16[81,384]{1,0:T(8,128)(2,1)S(1)}, u32[]{:S(2)}, u32[]{:S(2)}) collective-permute-start(bf16[81,384]{1,0:T(8,128)(2,1)S(1)} %slice.16), channel_id=1, source_target_pairs={{0,5},{1,6},{2,7},{3,8},{4,9},{5,10},{6,11},{7,12},{8,13},{9,14},{... | collective-permute-start | bytes 186632
Sparse Core Ops, SparseCore 0:
  9.4 114.7 all-gather.4
  126.3 93.6 all-gather.6
  222.0 82.1 all-gather.8
